TPU v7x, 256 devices: a whole 4x4x8 slice. The times are simulated.
256 devices in a mesh: isl: 16 (over z_lo, x), par: 2 (over z_hi), sp: 8 (over y, core).
Axes of the slice: x: 4, y: 4, z: 8 (z_hi: 2, z_lo: 4; z = z_hi * 4 + z_lo), core: 2. Of those that a mesh axis runs over, the one named last changes fastest.
Arguments:
- ensemble: float32 [16, 2, 4, 32, 32, 512], P('isl', 'par', None, 'sp'), may hold values from -6 to 6
- observations: float32 [32, 512], P('sp'), may hold values from -6 to 6
- obs_precision: float32 [32, 512], P('sp'), may hold values from 0.002 to 0.02
- island_ancestor: int32 [16], replicated, may hold values from 0 to 15, as said below
- particle_ancestor: int32 [16, 2], P('isl', 'par'), may hold values from 0 to 1, as said below
Outputs:
- resampled: float32 [16, 2, 4, 32, 32, 512], P('isl', 'par', None, 'sp')
- particle_logw: float32 [16, 2], P('isl', 'par')
- island_logw: float32 [16], P('isl')
Inputs may be any that keep to these rules, and one draw needn't show every extreme that they name: island_ancestor names island 16 - 1 and island 0 in every draw. Every row of particle_ancestor names particle 0 and particle 2 - 1.
All inputs are finite; a program needn't handle non-finite values.
Results may differ from a plain program's by a relative error of at most 0.000069.
Values sent between devices are 32-bit elements; how exact they have to be, the bound alone decides.
A program may use at most 64 MiB of HBM per device.

v0:
```python
import jax
import jax.numpy as jnp
from jax import lax
from jax.sharding import PartitionSpec as P

SWEEPS = 8
dt_step = 0.2
viscosity = 0.05
stratification = 1.0
relaxation = 0.8


def extended_2(cells, sides, width):
    for axis, dim in sides:
        count = lax.axis_size(axis)
        head = lax.slice_in_dim(cells, 0, width, axis=dim)
        tail = lax.slice_in_dim(cells, cells.shape[dim] - width, cells.shape[dim], axis=dim)
        cells = jnp.concatenate(
            [
                lax.ppermute(tail, axis, [(i, (i + 1) % count) for i in range(count)]),
                cells,
                lax.ppermute(head, axis, [((i + 1) % count, i) for i in range(count)]),
            ],
            axis=dim,
        )
    return cells


def pad_vertical(field, width):
    pad_widths = [(0, 0)] * field.ndim
    pad_widths[-2] = (width, width)
    return jnp.pad(field, pad_widths)


def fourth_north(field):
    return (
        8.0 * (jnp.roll(field, -1, -1) - jnp.roll(field, 1, -1))
        - (jnp.roll(field, -2, -1) - jnp.roll(field, 2, -1))
    ) / 12.0


def fourth_vertical(field):
    padded = pad_vertical(field, 2)
    return (
        8.0 * (padded[..., 3:-1, :] - padded[..., 1:-3, :])
        - (padded[..., 4:, :] - padded[..., :-4, :])
    ) / 12.0


def fourth_east(extended):
    return (
        8.0 * (extended[..., 3:-1, :, :] - extended[..., 1:-3, :, :])
        - (extended[..., 4:, :, :] - extended[..., :-4, :, :])
    ) / 12.0


def second_north(field):
    return 0.5 * (jnp.roll(field, -1, -1) - jnp.roll(field, 1, -1))


def second_vertical(field):
    padded = pad_vertical(field, 1)
    return 0.5 * (padded[..., 2:, :] - padded[..., :-2, :])


def centred_east(padded):
    return 0.5 * (padded[..., 2:, :, :] - padded[..., :-2, :, :])


def neighbours(padded):
    middle = padded[..., 1:-1, :, :]
    vertical = pad_vertical(middle, 1)
    return (
        padded[..., 2:, :, :]
        + padded[..., :-2, :, :]
        + jnp.roll(middle, 1, -1)
        + jnp.roll(middle, -1, -1)
        + vertical[..., 2:, :]
        + vertical[..., :-2, :]
    )


def tendency(extended, zonal, merid, vertical_flow):
    field = extended[..., 2:-2, :, :]
    laplace = neighbours(extended[..., 1:-1, :, :]) - 6.0 * field
    advect = (
        zonal * fourth_east(extended)
        + merid * fourth_north(field)
        + vertical_flow * fourth_vertical(field)
    )
    return viscosity * laplace - advect


def sweep(padded, divergence):
    middle = padded[..., 1:-1, :, :]
    return middle + relaxation * (neighbours(padded) - 6.0 * middle - divergence) / 6.0


def log_total(values, axis_index):
    upper_boundary = jnp.max(values, axis=axis_index, keepdims=True)
    return jnp.squeeze(upper_boundary, axis_index) + jnp.log(
        jnp.sum(jnp.exp(values - upper_boundary), axis=axis_index)
    )


def shards(ensemble, observations, obs_precision, island_ancestor, particle_ancestor):
    model_state = ensemble[0]
    rows_east = model_state.shape[2]
    island_now = lax.axis_index("isl")
    source_island = island_ancestor[island_now]
    picks = particle_ancestor[0]
    zonal = model_state[:, 0]
    merid = model_state[:, 1]
    vertical_flow = model_state[:, 2]
    buoyancy = model_state[:, 3]
    extended = extended_2(model_state, (("sp", 2),), 2)
    star_zonal = zonal + dt_step * tendency(extended[:, 0], zonal, merid, vertical_flow)
    star_merid = merid + dt_step * tendency(extended[:, 1], zonal, merid, vertical_flow)
    star_vertical = vertical_flow + dt_step * (
        tendency(extended[:, 2], zonal, merid, vertical_flow) + buoyancy
    )
    buoyancy_provisional_tendency = buoyancy + dt_step * (
        tendency(extended[:, 3], zonal, merid, vertical_flow) - stratification * vertical_flow
    )
    zonal_wide = extended_2(star_zonal, (("sp", 1),), 1)
    divergence = (
        centred_east(zonal_wide) + second_north(star_merid) + second_vertical(star_vertical)
    )
    potential = -relaxation * divergence / 6.0
    for repeat_index in range(SWEEPS):
        padded = extended_2(potential, (("sp", 1),), 1)
        potential = sweep(padded, divergence)
    padded = extended_2(potential, (("sp", 1),), 1)
    stepped = jnp.stack(
        [
            star_zonal - centred_east(padded),
            star_merid - second_north(potential),
            star_vertical - second_vertical(potential),
            buoyancy_provisional_tendency,
        ],
        axis=1,
    )
    upper_boundary = stepped[:, 3][:, :, -1, :]
    nx_total = lax.axis_size("sp") * rows_east
    positions = (lax.axis_index("sp") * rows_east + jnp.arange(rows_east, dtype=jnp.int32)).astype(
        jnp.float32
    )
    ramp = 1.0 + positions * (2.0 / (nx_total - 1))
    scale = obs_precision * ramp[:, None]
    partial_value = jnp.sum((upper_boundary - observations) ** 2 * scale, axis=(1, 2))
    misfit = lax.psum(partial_value, "sp")
    log_weight = -0.5 * misfit
    island_weights = lax.all_gather(log_weight, "par", axis=0, tiled=True)
    island_total = log_total(island_weights, 0)
    particle_out = log_weight - island_total
    totals = lax.all_gather(island_total[None], "isl", axis=0, tiled=True)
    island_out = island_total - log_total(totals, 0)
    particle_out, island_out = (particle_out, island_out)
    piece = lax.all_gather(stepped[None], "isl", axis=0, tiled=True)
    labels = jnp.arange(piece.shape[0], dtype=jnp.int32)
    matched = (labels == source_island)[:, None, None, None, None, None]
    copied = jnp.sum(jnp.where(matched, piece, 0.0), axis=0, keepdims=True)
    complete_island_state = lax.all_gather(copied, "par", axis=1, tiled=True)
    result = jnp.take(complete_island_state[0], picks, axis=0)
    return (result[None], particle_out[None], island_out[None])


def solution(mesh):
    return jax.shard_map(
        shards,
        mesh=mesh,
        in_specs=(
            P("isl", "par", None, "sp", None, None),
            P("sp", None),
            P("sp", None),
            P(),
            P("isl", "par"),
        ),
        out_specs=(P("isl", "par", None, "sp", None, None), P("isl", "par"), P("isl")),
        check_vma=False,
    )
```

profile of v0, /device:TPU:128, one launch (start us, length us, event | category | flops | bytes accessed | tf_op | source)
XLA Modules:
  0.0 370.2 jit_solution(13943572929849867741)
XLA Ops:
  7.2 1.4 fusion.178
  8.6 2.9 collective-permute-start.1
  11.6 6.9 %collective-permute-done = f32[1,4,2,32,512]{4,3,2,1,0:T(8,128)S(1)} collective-permute-done((f32[1,4,2,32,512]{4,3,2,1,0:T(8,128)S(1)}, f32[1,4,2,32,512]{4,3,2,1,0:T(8,128)S(1)}, u32[]{:S(2)}, u32[]{:S(2)}) %collective-permute-start) | collective-permute-done | bytes 524320 | tf_op jit(solution)/shard_map/ppermute | solution.py:20
  18.6 0.3 slice_bitcast_fusion.3
  19.2 0.2 fusion.190
  20.3 0.5 fusion.14
  20.9 0.5 fusion.7
  21.4 3.0 collective-permute-start.2
  24.3 0.5 fusion.84
  24.8 0.5 fusion.22
  25.3 0.9 collective-permute-done.2
  26.2 3.0 collective-permute-done.3
  29.6 0.5 collective-permute-start.5
  30.2 1.3 collective-permute-done.4
  31.5 3.0 collective-permute-done.5
  34.9 0.5 collective-permute-start.7
  35.5 1.3 collective-permute-done.6
  36.8 3.0 collective-permute-done.7
  39.8 0.2 fusion.36
  40.2 0.5 collective-permute-start.9
  40.8 1.3 collective-permute-done.8
  42.1 3.0 collective-permute-done.9
  45.1 0.2 fusion.42
  45.5 0.5 collective-permute-start.11
  46.1 1.3 collective-permute-done.10
  47.4 3.0 collective-permute-done.11
  50.4 0.2 fusion.48
  50.8 0.5 collective-permute-start.13
  51.4 1.3 collective-permute-done.12
  52.7 3.0 collective-permute-done.13
  55.8 0.2 fusion.54
  56.2 0.5 collective-permute-start.15
  56.7 1.3 collective-permute-done.14
  58.1 3.0 collective-permute-done.15
  61.1 0.2 fusion.60
  61.5 0.5 collective-permute-start.17
  62.1 1.3 collective-permute-done.16
  63.4 3.0 collective-permute-done.17
  66.4 0.2 fusion.66
  66.8 0.5 collective-permute-start.19
  67.4 1.3 collective-permute-done.18
  68.7 3.0 collective-permute-done.19
  71.7 0.2 fusion.72
  72.2 0.5 collective-permute-start.21
  72.9 1.2 collective-permute-done.20
  74.1 3.0 collective-permute-done.21
  77.2 1.1 pad_maximum_fusion.1
  78.4 0.6 dynamic_slice.3
  78.9 0.6 iota_compare_fusion
  79.7 181.6 %all-gather.5.cloned.1.call-done = f32[16,4,4,32,512]{4,3,2,1,0:T(8,128)} async-done(((f32[1,4,4,32,512]{4,3,2,1,0:T(8,128)}), f32[16,4,4,32,512]{4,3,2,1,0:T(8,128)}) %all-gather.5.cloned.1.call-update) | async-done | bytes 16777232 | tf_op jit(solution)/shard_map/all_gather | solution.py:159
  261.3 9.1 %fusion = f32[4,4,32,512]{3,2,1,0:T(8,128)} fusion(f32[16,4,4,32,512]{4,3,2,1,0:T(8,128)} %all-gather.5.cloned.1.call-done, pred[16]{0:T(512)(128)(4,1)S(1)} %iota_compare_fusion), kind=kLoop, calls=%fused_computation.1 | loop fusion | flops 8126464 | bytes 17825808 | tf_op jit(solution)/shard_map/reduce_sum | solution.py:162
  270.4 0.6 dynamic-slice.5
  271.0 0.6 dynamic-slice.6
  272.3 0.7 fusion.176
  273.0 15.0 %psum.7 = f32[1]{0:T(128)} all-reduce(f32[1]{0:T(128)} %bitcast.19), channel_id=1, replica_groups=mesh['isl'=16,'par'=2,'sp'=8] {'sp'}, use_global_device_ids=true, to_apply=%region_2.3 | all-reduce | flops 1 | bytes 8 | tf_op jit(solution)/shard_map/psum | solution.py:151
  288.0 1.4 multiply_dynamic-update-slice_fusion
  289.4 11.1 %all-reduce.18 = f32[2]{0:T(128)S(1)} all-reduce(f32[2]{0:T(128)S(1)} %multiply_dynamic-update-slice_fusion), channel_id=1, replica_groups=mesh['isl'=16,'par'=2,'sp'=8] {'par'}, use_global_device_ids=true, to_apply=%add.18 | all-reduce | flops 2 | bytes 16
  300.5 0.6 reduce_max.18
  301.1 1.3 exponential_reduce_fusion.1
  303.7 0.7 dynamic-update-slice.2
  304.4 50.6 %all-reduce.19 = f32[16]{0:T(128)S(1)} all-reduce(f32[16]{0:T(128)S(1)} %dynamic-update-slice.2), channel_id=1, replica_groups=mesh['isl'=16,'par'=2,'sp'=8] {'isl'}, use_global_device_ids=true, to_apply=%add.19 | all-reduce | flops 16 | bytes 128
  355.0 0.6 reduce_max.19
  355.6 1.2 exponential_reduce_fusion
  358.8 2.3 dynamic-slice_select_fusion
  (79 shorter events, 4.6 us)
Async XLA Ops:
  7.2 11.3 %copy-start = (f32[1,1,4,4,32,512]{5,4,3,2,1,0:T(8,128)S(1)}, f32[1,1,4,4,32,512]{5,4,3,2,1,0:T(8,128)}, u32[]{:S(2)}) copy-start(f32[1,1,4,4,32,512]{5,4,3,2,1,0:T(8,128)} %param.5) | copy-start | bytes 3145732
  7.2 254.1 %all-gather.5.cloned.1.call-start = ((), (), s32[]{:S(2)}) async-start(), calls=%async_computation | async-start | bytes 17825792 | tf_op jit(solution)/shard_map/all_gather | solution.py:159
  8.6 9.8 %collective-permute-start = (f32[1,4,2,32,512]{4,3,2,1,0:T(8,128)S(1)}, f32[1,4,2,32,512]{4,3,2,1,0:T(8,128)S(1)}, u32[]{:S(2)}, u32[]{:S(2)}) collective-permute-start(f32[1,4,2,32,512]{4,3,2,1,0:T(8,128)S(1)} %get-tuple-element.20), channel_id=1, source_target_pairs={{0,1},{1,2},{2,3},{3,4},{4,5},{5,6},{6,7},{7,0},{8,9},{9,10},{10,1... | collective-permute-start | bytes 1572872 | tf_op jit(solution)/shard_map/ppermute | solution.py:20
  8.6 9.8 %collective-permute-start.1 = (f32[1,4,2,32,512]{4,3,2,1,0:T(8,128)S(1)}, f32[1,4,2,32,512]{4,3,2,1,0:T(8,128)S(1)}, u32[]{:S(2)}, u32[]{:S(2)}) collective-permute-start(f32[1,4,2,32,512]{4,3,2,1,0:T(8,128)S(1)} %get-tuple-element.21), channel_id=1, source_target_pairs={{1,0},{2,1},{3,2},{4,3},{5,4},{6,5},{7,6},{0,7},{9,8},{10,9},{11,1... | collective-permute-start | bytes 1572872 | tf_op jit(solution)/shard_map/ppermute | solution.py:22
  21.4 4.9 %collective-permute-start.2 = (f32[1,1,32,512]{3,2,1,0:T(8,128)S(1)}, f32[1,1,32,512]{3,2,1,0:T(8,128)S(1)}, u32[]{:S(2)}, u32[]{:S(2)}) collective-permute-start(f32[1,1,32,512]{3,2,1,0:T(8,128)S(1)} %get-tuple-element.110), channel_id=1, source_target_pairs={{1,0},{2,1},{3,2},{4,3},{5,4},{6,5},{7,6},{0,7},{9,8},{10,9},{11,1... | collective-permute-start | bytes 196616 | tf_op jit(solution)/shard_map/ppermute | solution.py:22
  24.3 4.9 %collective-permute-start.3 = (f32[1,1,32,512]{3,2,1,0:T(8,128)S(1)}, f32[1,1,32,512]{3,2,1,0:T(8,128)S(1)}, u32[]{:S(2)}, u32[]{:S(2)}) collective-permute-start(f32[1,1,32,512]{3,2,1,0:T(8,128)S(1)} %get-tuple-element.111), channel_id=1, source_target_pairs={{0,1},{1,2},{2,3},{3,4},{4,5},{5,6},{6,7},{7,0},{8,9},{9,10},{10,1... | collective-permute-start | bytes 196616 | tf_op jit(solution)/shard_map/ppermute | solution.py:20
  29.6 1.9 collective-permute-start.4
  29.6 4.9 %collective-permute-start.5 = (f32[1,1,32,512]{3,2,1,0:T(8,128)S(1)}, f32[1,1,32,512]{3,2,1,0:T(8,128)S(1)}, u32[]{:S(2)}, u32[]{:S(2)}) collective-permute-start(f32[1,1,32,512]{3,2,1,0:T(8,128)S(1)} %get-tuple-element.109), channel_id=1, source_target_pairs={{0,1},{1,2},{2,3},{3,4},{4,5},{5,6},{6,7},{7,0},{8,9},{9,10},{10,1... | collective-permute-start | bytes 196616 | tf_op jit(solution)/shard_map/ppermute | solution.py:20
  34.9 1.9 collective-permute-start.6
  34.9 4.9 %collective-permute-start.7 = (f32[1,1,32,512]{3,2,1,0:T(8,128)S(1)}, f32[1,1,32,512]{3,2,1,0:T(8,128)S(1)}, u32[]{:S(2)}, u32[]{:S(2)}) collective-permute-start(f32[1,1,32,512]{3,2,1,0:T(8,128)S(1)} %get-tuple-element.103), channel_id=1, source_target_pairs={{0,1},{1,2},{2,3},{3,4},{4,5},{5,6},{6,7},{7,0},{8,9},{9,10},{10,1... | collective-permute-start | bytes 196616 | tf_op jit(solution)/shard_map/ppermute | solution.py:20
  40.2 1.9 collective-permute-start.8
  40.2 4.9 %collective-permute-start.9 = (f32[1,1,32,512]{3,2,1,0:T(8,128)S(1)}, f32[1,1,32,512]{3,2,1,0:T(8,128)S(1)}, u32[]{:S(2)}, u32[]{:S(2)}) collective-permute-start(f32[1,1,32,512]{3,2,1,0:T(8,128)S(1)} %get-tuple-element.97), channel_id=1, source_target_pairs={{0,1},{1,2},{2,3},{3,4},{4,5},{5,6},{6,7},{7,0},{8,9},{9,10},{10,1... | collective-permute-start | bytes 196616 | tf_op jit(solution)/shard_map/ppermute | solution.py:20
  45.5 1.9 collective-permute-start.10
  45.5 4.9 %collective-permute-start.11 = (f32[1,1,32,512]{3,2,1,0:T(8,128)S(1)}, f32[1,1,32,512]{3,2,1,0:T(8,128)S(1)}, u32[]{:S(2)}, u32[]{:S(2)}) collective-permute-start(f32[1,1,32,512]{3,2,1,0:T(8,128)S(1)} %get-tuple-element.91), channel_id=1, source_target_pairs={{0,1},{1,2},{2,3},{3,4},{4,5},{5,6},{6,7},{7,0},{8,9},{9,10},{10,1... | collective-permute-start | bytes 196616 | tf_op jit(solution)/shard_map/ppermute | solution.py:20
  50.8 1.9 collective-permute-start.12
  50.8 4.9 %collective-permute-start.13 = (f32[1,1,32,512]{3,2,1,0:T(8,128)S(1)}, f32[1,1,32,512]{3,2,1,0:T(8,128)S(1)}, u32[]{:S(2)}, u32[]{:S(2)}) collective-permute-start(f32[1,1,32,512]{3,2,1,0:T(8,128)S(1)} %get-tuple-element.85), channel_id=1, source_target_pairs={{0,1},{1,2},{2,3},{3,4},{4,5},{5,6},{6,7},{7,0},{8,9},{9,10},{10,1... | collective-permute-start | bytes 196616 | tf_op jit(solution)/shard_map/ppermute | solution.py:20
  56.1 1.9 collective-permute-start.14
  56.2 4.9 %collective-permute-start.15 = (f32[1,1,32,512]{3,2,1,0:T(8,128)S(1)}, f32[1,1,32,512]{3,2,1,0:T(8,128)S(1)}, u32[]{:S(2)}, u32[]{:S(2)}) collective-permute-start(f32[1,1,32,512]{3,2,1,0:T(8,128)S(1)} %get-tuple-element.79), channel_id=1, source_target_pairs={{0,1},{1,2},{2,3},{3,4},{4,5},{5,6},{6,7},{7,0},{8,9},{9,10},{10,1... | collective-permute-start | bytes 196616 | tf_op jit(solution)/shard_map/ppermute | solution.py:20
  61.5 1.9 collective-permute-start.16
  61.5 4.9 %collective-permute-start.17 = (f32[1,1,32,512]{3,2,1,0:T(8,128)S(1)}, f32[1,1,32,512]{3,2,1,0:T(8,128)S(1)}, u32[]{:S(2)}, u32[]{:S(2)}) collective-permute-start(f32[1,1,32,512]{3,2,1,0:T(8,128)S(1)} %get-tuple-element.73), channel_id=1, source_target_pairs={{0,1},{1,2},{2,3},{3,4},{4,5},{5,6},{6,7},{7,0},{8,9},{9,10},{10,1... | collective-permute-start | bytes 196616 | tf_op jit(solution)/shard_map/ppermute | solution.py:20
  66.8 1.9 collective-permute-start.18
  66.8 4.9 %collective-permute-start.19 = (f32[1,1,32,512]{3,2,1,0:T(8,128)S(1)}, f32[1,1,32,512]{3,2,1,0:T(8,128)S(1)}, u32[]{:S(2)}, u32[]{:S(2)}) collective-permute-start(f32[1,1,32,512]{3,2,1,0:T(8,128)S(1)} %get-tuple-element.67), channel_id=1, source_target_pairs={{0,1},{1,2},{2,3},{3,4},{4,5},{5,6},{6,7},{7,0},{8,9},{9,10},{10,1... | collective-permute-start | bytes 196616 | tf_op jit(solution)/shard_map/ppermute | solution.py:20
  72.2 1.9 collective-permute-start.20
  72.2 4.9 %collective-permute-start.21 = (f32[1,1,32,512]{3,2,1,0:T(8,128)S(1)}, f32[1,1,32,512]{3,2,1,0:T(8,128)S(1)}, u32[]{:S(2)}, u32[]{:S(2)}) collective-permute-start(f32[1,1,32,512]{3,2,1,0:T(8,128)S(1)} %get-tuple-element.57), channel_id=1, source_target_pairs={{0,1},{1,2},{2,3},{3,4},{4,5},{5,6},{6,7},{7,0},{8,9},{9,10},{10,1... | collective-permute-start | bytes 196616 | tf_op jit(solution)/shard_map/ppermute | solution.py:20
  72.9 5.5 %copy-start.3 = (s32[16]{0:T(128)S(1)}, s32[16]{0:T(128)}, u32[]{:S(2)}) copy-start(s32[16]{0:T(128)} %param.8) | copy-start | bytes 196
  78.3 280.5 %all-gather.7.cloned.1.call-start = ((), (), s32[]{:S(2)}) async-start(), calls=%async_computation.1 | async-start | bytes 3145728 | tf_op jit(solution)/shard_map/all_gather | solution.py:163
  79.6 190.8 %copy-start.5 = (u32[256]{0:T(256)S(1)}, u32[256]{0:T(256)}, u32[]{:S(2)}) copy-start(u32[256]{0:T(256)} %constant.156) | copy-start | bytes 3076
  79.6 191.4 %copy-start.4 = (u32[256]{0:T(256)S(1)}, u32[256]{0:T(256)}, u32[]{:S(2)}) copy-start(u32[256]{0:T(256)} %constant.161) | copy-start | bytes 3076
  79.6 192.6 %copy-start.1 = (f32[4,512]{1,0:T(4,128)S(1)}, f32[4,512]{1,0:T(4,128)}, u32[]{:S(2)}) copy-start(f32[4,512]{1,0:T(4,128)} %param.6) | copy-start | bytes 24580
  79.6 192.6 %copy-start.2 = (f32[4,512]{1,0:T(4,128)S(1)}, f32[4,512]{1,0:T(4,128)}, u32[]{:S(2)}) copy-start(f32[4,512]{1,0:T(4,128)} %param.7) | copy-start | bytes 24580
Sparse Core Ops, SparseCore 0:
  78.4 182.8 all-gather.4
  270.5 58.8 all-gather.6
where the time goes:
time: 371 us; the launch traced here: 370 us
  waiting for transfers between devices  231 us (62%)
  blocking collectives  76.8 us (21%)
  other arithmetic  23.1 us (6%)
  between operations  20.7 us (6%)
  starting transfers between devices  10.6 us (3%)
  local copies, waits for them, and re-layouts  7.69 us (2%)
    all_gather x1, waiting for transfers between devices, shards(): piece = lax.all_gather(stepped[None], 'isl', axis=0, tiled=True)  182 us
    unnamed x2, blocking collectives  61.7 us
    ppermute x11, waiting for transfers between devices, extended_2(): lax.ppermute(tail, axis, [(i, (i + 1) % count) for i in range(count)])  37 us
    psum x1, blocking collectives, shards(): misfit = lax.psum(partial_value, 'sp')  15 us
    ppermute x11, waiting for transfers between devices, extended_2(): lax.ppermute(head, axis, [((i + 1) % count, i) for i in range(count)])  12.7 us
    reduce_sum x1, other arithmetic, shards(): copied = jnp.sum(jnp.where(matched, piece, 0.0), axis=0, keepdims=True)  9.07 us
  transfers between devices with their start and end apart: 24, of which 22 were waited for; matrix products, arithmetic and copies ran while one was open for 3% of the time, Pallas kernels for 0%

commit v1 on v0

--- a/solution.py
+++ b/solution.py
@@ -156,7 +156,9 @@
     totals = lax.all_gather(island_total[None], "isl", axis=0, tiled=True)
     island_out = island_total - log_total(totals, 0)
     particle_out, island_out = (particle_out, island_out)
-    piece = lax.all_gather(stepped[None], "isl", axis=0, tiled=True)
+    piece = jnp.concatenate(
+        lax.all_to_all(jnp.stack([stepped[None]] * lax.axis_size("isl")), "isl", 0, 0), axis=0
+    )
     labels = jnp.arange(piece.shape[0], dtype=jnp.int32)
     matched = (labels == source_island)[:, None, None, None, None, None]
     copied = jnp.sum(jnp.where(matched, piece, 0.0), axis=0, keepdims=True)

time: 371 us -> 564 us (1.52)
  waiting for transfers between devices: 231 us -> 343 us
  blocking collectives: 76.8 us -> 132 us
  local copies, waits for them, and re-layouts: 7.69 us -> 20 us
  starting transfers between devices: 10.6 us -> 16.6 us
    all_to_all x0 -> x1, waiting for transfers between devices: none -> 295 us  [shards(): lax.all_to_all(jnp.stack([stepped[None]] * lax.axis_size('isl')), 'isl',...]
    all_gather x1 -> x0, waiting for transfers between devices: 182 us -> none  [shards(): piece = lax.all_gather(stepped[None], 'isl', axis=0, tiled=True)]
    unnamed x2, blocking collectives: 61.7 us -> 119 us
    another operation x0 -> x2, local copies, waits for them, and re-layouts: none -> 8.22 us  [the longest x1 7.9 us: shards(): jnp.stack([stepped[None]] * lax.axis_size('isl'))]
    all_to_all x0 -> x1, starting transfers between devices: none -> 5.95 us  [shards(): lax.all_to_all(jnp.stack([stepped[None]] * lax.axis_size('isl')), 'isl',...]
  transfers between devices with their start and end apart: 24 -> 24, of which waited for: 22 -> 21; matrix products, arithmetic and copies ran while one was open for 3% -> 2% of each run, Pallas kernels for 0% -> 0%
where the time goes in v1:
time: 564 us; the launch traced here: 560 us
  waiting for transfers between devices  343 us (61%)
  blocking collectives  132 us (23%)
  other arithmetic  27.4 us (5%)
  between operations  20.7 us (4%)
  local copies, waits for them, and re-layouts  20 us (4%)
  starting transfers between devices  16.6 us (3%)
    all_to_all x1, waiting for transfers between devices, shards(): lax.all_to_all(jnp.stack([stepped[None]] * lax.axis_size('isl')), 'isl',...  295 us
    unnamed x2, blocking collectives  119 us
    ppermute x11, waiting for transfers between devices, extended_2(): lax.ppermute(tail, axis, [(i, (i + 1) % count) for i in range(count)])  37 us
    psum x1, blocking collectives, shards(): misfit = lax.psum(partial_value, 'sp')  13.2 us
    ppermute x11, waiting for transfers between devices, extended_2(): lax.ppermute(head, axis, [((i + 1) % count, i) for i in range(count)])  11.6 us
  transfers between devices with their start and end apart: 24, of which 21 were waited for; matrix products, arithmetic and copies ran while one was open for 2% of the time, Pallas kernels for 0%

profile of v1, /device:TPU:128, one launch (start us, length us, event | category | flops | bytes accessed | tf_op | source)
XLA Modules:
  0.0 560.1 jit_solution(3402515878315127581)
XLA Ops:
  7.2 1.9 copy.13
  9.5 2.9 collective-permute-start.1
  12.5 6.9 %collective-permute-done = f32[1,4,2,32,512]{4,2,3,1,0:T(2,128)S(1)} collective-permute-done((f32[1,4,2,32,512]{4,2,3,1,0:T(2,128)S(1)}, f32[1,4,2,32,512]{4,2,3,1,0:T(2,128)S(1)}, u32[]{:S(2)}, u32[]{:S(2)}) %collective-permute-start) | collective-permute-done | bytes 524320 | tf_op jit(solution)/shard_map/ppermute | solution.py:20
  19.3 0.7 pad_maximum_fusion
  22.8 0.9 fusion.82
  23.8 0.9 fusion.93
  24.8 3.0 collective-permute-start.2
  27.8 0.9 multiply_add_fusion
  28.7 0.9 multiply_add_fusion.9
  29.7 3.0 collective-permute-done.3
  33.5 0.5 collective-permute-start.5
  34.1 1.3 collective-permute-done.4
  35.4 3.0 collective-permute-done.5
  38.4 0.5 multiply_add_fusion.8
  39.2 0.5 collective-permute-start.7
  39.8 1.3 collective-permute-done.6
  41.1 3.0 collective-permute-done.7
  44.2 0.5 multiply_add_fusion.7
  45.0 0.5 collective-permute-start.9
  45.6 1.3 collective-permute-done.8
  46.9 3.0 collective-permute-done.9
  49.9 0.5 multiply_add_fusion.6
  51.0 0.5 collective-permute-start.11
  51.6 1.3 collective-permute-done.10
  52.9 3.0 collective-permute-done.11
  55.9 0.5 multiply_add_fusion.5
  56.8 0.5 collective-permute-start.13
  57.4 1.3 collective-permute-done.12
  58.7 3.0 collective-permute-done.13
  61.7 0.5 multiply_add_fusion.4
  62.5 0.5 collective-permute-start.15
  63.1 1.3 collective-permute-done.14
  64.4 3.0 collective-permute-done.15
  67.5 0.5 multiply_add_fusion.3
  68.3 0.5 collective-permute-start.17
  68.9 1.3 collective-permute-done.16
  70.2 3.0 collective-permute-done.17
  73.2 0.5 multiply_add_fusion.2
  74.1 0.5 collective-permute-start.19
  74.7 1.3 collective-permute-done.18
  76.0 3.0 collective-permute-done.19
  79.0 0.5 multiply_add_fusion.1
  80.0 0.5 collective-permute-start.21
  80.8 1.1 collective-permute-done.20
  81.9 3.0 collective-permute-done.21
  85.8 7.9 %stack.26 = f32[16,1,1,4,4,32,512]{6,5,4,3,2,1,0:T(8,128)} broadcast(f32[4,4,32,512]{3,2,1,0:T(8,128)S(1)} %copy.11), dimensions={3,4,5,6} | broadcast | bytes 17825792 | tf_op jit(solution)/shard_map/stack | solution.py:160
  93.7 6.0 %all-to-all-start = ((f32[16,1,1,4,4,32,512]{6,5,4,3,2,1,0:T(8,128)}), f32[16,1,1,4,4,32,512]{6,5,4,3,2,1,0:T(8,128)}, u32[]{:S(2)}, u32[]{:S(2)}) async-start(f32[16,1,1,4,4,32,512]{6,5,4,3,2,1,0:T(8,128)} %stack.26), calls=%async_computation | async-start | bytes 33554432 | tf_op jit(solution)/shard_map/all_to_all | solution.py:160
  99.7 0.6 dynamic_slice.3
  100.3 0.6 iota_compare_fusion
  101.0 294.5 %all-to-all-done = f32[16,1,1,4,4,32,512]{6,5,4,3,2,1,0:T(8,128)} async-done(((f32[16,1,1,4,4,32,512]{6,5,4,3,2,1,0:T(8,128)}), f32[16,1,1,4,4,32,512]{6,5,4,3,2,1,0:T(8,128)}, u32[]{:S(2)}, u32[]{:S(2)}) %all-to-all-start) | async-done | bytes 16777248 | tf_op jit(solution)/shard_map/all_to_all | solution.py:160
  395.6 9.1 %fusion = f32[4,4,32,512]{3,2,1,0:T(8,128)} fusion(f32[16,1,1,4,4,32,512]{6,5,4,3,2,1,0:T(8,128)} %all-to-all-done, pred[16]{0:T(512)(128)(4,1)S(1)} %iota_compare_fusion), kind=kLoop, calls=%fused_computation.1 | loop fusion | flops 8126464 | bytes 17825808 | tf_op jit(solution)/shard_map/reduce_sum | solution.py:164
  404.7 0.6 dynamic-slice.5
  405.3 0.6 dynamic-slice.6
  406.6 0.7 fusion.112
  407.3 13.2 %psum.7 = f32[1]{0:T(128)} all-reduce(f32[1]{0:T(128)} %bitcast.21), channel_id=1, replica_groups=mesh['isl'=16,'par'=2,'sp'=8] {'sp'}, use_global_device_ids=true, to_apply=%region_2.3 | all-reduce | flops 1 | bytes 8 | tf_op jit(solution)/shard_map/psum | solution.py:151
  420.4 1.3 multiply_dynamic-update-slice_fusion
  421.7 8.9 %all-reduce.18 = f32[2]{0:T(128)S(1)} all-reduce(f32[2]{0:T(128)S(1)} %multiply_dynamic-update-slice_fusion), channel_id=1, replica_groups=mesh['isl'=16,'par'=2,'sp'=8] {'par'}, use_global_device_ids=true, to_apply=%add.18 | all-reduce | flops 2 | bytes 16
  430.7 0.6 reduce_max.18
  431.3 1.3 exponential_reduce_fusion.1
  433.9 0.7 dynamic-update-slice.2
  434.6 110.2 %all-reduce.19 = f32[16]{0:T(128)S(1)} all-reduce(f32[16]{0:T(128)S(1)} %dynamic-update-slice.2), channel_id=1, replica_groups=mesh['isl'=16,'par'=2,'sp'=8] {'isl'}, use_global_device_ids=true, to_apply=%add.19 | all-reduce | flops 16 | bytes 128
  544.8 0.6 reduce_max.19
  545.4 1.3 exponential_reduce_fusion
  548.7 2.3 dynamic-slice_select_fusion
  (78 shorter events, 9.2 us)
Async XLA Ops:
  9.5 9.8 %collective-permute-start = (f32[1,4,2,32,512]{4,2,3,1,0:T(2,128)S(1)}, f32[1,4,2,32,512]{4,2,3,1,0:T(2,128)S(1)}, u32[]{:S(2)}, u32[]{:S(2)}) collective-permute-start(f32[1,4,2,32,512]{4,2,3,1,0:T(2,128)S(1)} %get-tuple-element.20), channel_id=1, source_target_pairs={{0,1},{1,2},{2,3},{3,4},{4,5},{5,6},{6,7},{7,0},{8,9},{9,10},{10,1... | collective-permute-start | bytes 1572872 | tf_op jit(solution)/shard_map/ppermute | solution.py:20
  9.5 9.8 %collective-permute-start.1 = (f32[1,4,2,32,512]{4,2,3,1,0:T(2,128)S(1)}, f32[1,4,2,32,512]{4,2,3,1,0:T(2,128)S(1)}, u32[]{:S(2)}, u32[]{:S(2)}) collective-permute-start(f32[1,4,2,32,512]{4,2,3,1,0:T(2,128)S(1)} %get-tuple-element.21), channel_id=1, source_target_pairs={{1,0},{2,1},{3,2},{4,3},{5,4},{6,5},{7,6},{0,7},{9,8},{10,9},{11,1... | collective-permute-start | bytes 1572872 | tf_op jit(solution)/shard_map/ppermute | solution.py:22
  24.8 4.9 collective-permute-start.2
  27.8 4.9 collective-permute-start.3
  33.5 1.9 collective-permute-start.4
  33.5 4.9 collective-permute-start.5
  39.2 1.9 collective-permute-start.6
  39.2 4.9 collective-permute-start.7
  45.0 1.9 collective-permute-start.8
  45.0 4.9 collective-permute-start.9
  51.0 1.9 collective-permute-start.10
  51.0 4.9 collective-permute-start.11
  56.7 1.9 collective-permute-start.12
  56.8 4.9 collective-permute-start.13
  62.5 1.9 collective-permute-start.14
  62.5 4.9 collective-permute-start.15
  68.3 1.9 collective-permute-start.16
  68.3 4.9 collective-permute-start.17
  74.1 1.9 collective-permute-start.18
  74.1 4.9 collective-permute-start.19
  80.0 1.9 collective-permute-start.20
  80.0 4.9 collective-permute-start.21
  93.7 6.0 %copy-start.2 = (s32[16]{0:T(128)S(1)}, s32[16]{0:T(128)}, u32[]{:S(2)}) copy-start(s32[16]{0:T(128)} %param.8) | copy-start | bytes 196
  93.7 301.9 %all-to-all-start = ((f32[16,1,1,4,4,32,512]{6,5,4,3,2,1,0:T(8,128)}), f32[16,1,1,4,4,32,512]{6,5,4,3,2,1,0:T(8,128)}, u32[]{:S(2)}, u32[]{:S(2)}) async-start(f32[16,1,1,4,4,32,512]{6,5,4,3,2,1,0:T(8,128)} %stack.26), calls=%async_computation | async-start | bytes 33554432 | tf_op jit(solution)/shard_map/all_to_all | solution.py:160
  99.7 449.0 %all-gather.3.cloned.1.call-start = ((), (), s32[]{:S(2)}) async-start(), calls=%async_computation.1 | async-start | bytes 3145728 | tf_op jit(solution)/shard_map/all_gather | solution.py:165
  101.0 303.7 %copy-start.4 = (u32[256]{0:T(256)S(1)}, u32[256]{0:T(256)}, u32[]{:S(2)}) copy-start(u32[256]{0:T(256)} %constant.156) | copy-start | bytes 3076
  101.0 304.3 %copy-start.3 = (u32[256]{0:T(256)S(1)}, u32[256]{0:T(256)}, u32[]{:S(2)}) copy-start(u32[256]{0:T(256)} %constant.161) | copy-start | bytes 3076
  101.0 305.6 %copy-start = (f32[4,512]{1,0:T(4,128)S(1)}, f32[4,512]{1,0:T(4,128)}, u32[]{:S(2)}) copy-start(f32[4,512]{1,0:T(4,128)} %param.6) | copy-start | bytes 24580
  101.0 305.6 %copy-start.1 = (f32[4,512]{1,0:T(4,128)S(1)}, f32[4,512]{1,0:T(4,128)}, u32[]{:S(2)}) copy-start(f32[4,512]{1,0:T(4,128)} %param.7) | copy-start | bytes 24580
Sparse Core Ops, SparseCore 0:
  404.8 122.0 all-gather.2
